TPU v7x, 32 devices: a whole 2x2x4 slice. The times are simulated.
32 devices in a mesh: cl: 8 (over z, x), grp: 4 (over y, core).
Axes of the slice: x: 2, y: 2, z: 4, core: 2. Of those that a mesh axis runs over, the one named last changes fastest.
Arguments:
- basis: float32 [16, 4, 64, 128], P(None, 'grp', 'cl'), may hold values from -6 to 6
- near_blocks: bfloat16 [4, 64, 4, 128, 128], P('grp', 'cl'), may hold values from -0.25 to 0.25
- near_list: int32 [4, 64, 4], P('grp', 'cl'), may hold values from 0 to 23
- source_basis: bfloat16 [4, 64, 32, 128], P('grp', 'cl'), may hold values from -0.5 to 0.5
- target_basis: bfloat16 [4, 64, 32, 128], P('grp', 'cl'), may hold values from -1 to 1
- coupling: bfloat16 [4, 128, 1024], P('grp', 'cl'), may hold values from -0.75 to 0.75
- far_target: int32 [4, 128], P('grp'), may hold values from 0 to 63, as said below
- far_source: int32 [4, 128], P('grp', 'cl'), may hold values from 0 to 63, as said below
- far_count: int32 [4, 8], P('grp', 'cl'), may hold values from 8 to 16
Outputs:
- next_vector: float32 [4, 64, 128], P('grp', 'cl')
- hessenberg: float32 [17], replicated
Inputs may be any that keep to these rules, and one draw needn't show every extreme that they name: `far_target`: slots are owned in blocks of 16, block d by owner d of the group, whose clusters are d * 8 to (d + 1) * 8 - 1. Except for slot 1 of each owner, a slot's target lies within 16 clusters before or 23 after the owner's first cluster. Slot 1's target is a cluster of owner (d + 4) % 8. `far_source`: except for slot 0 of each owner, a slot's source lies within 80 clusters before or 87 after the owner's first cluster, and where the slot's target obeys the rule above the source differs from it by 16 to 64 clusters. Slot 0's source is a cluster of owner (d + 4) % 8.
All inputs are finite; a program needn't handle non-finite values.
Results may differ from a plain program's by a relative error of at most 0.0039.
Values may be sent and summed in bfloat16 or wider, within the bound.
A program may use at most 64 MiB of HBM per device.

v0:
```python
import jax
import jax.numpy as jnp
from jax import lax
from jax.sharding import PartitionSpec as P


def with_halo(cells, sides, width):
    for axis, dim in sides:
        count = lax.axis_size(axis)
        ends = count - 1
        head = lax.slice_in_dim(cells, 0, width, axis=dim)
        tail = lax.slice_in_dim(cells, cells.shape[dim] - width, cells.shape[dim], axis=dim)
        cells = jnp.concatenate(
            [
                lax.ppermute(tail, axis, [(i, (i + 1) % count) for i in range(ends)]),
                cells,
                lax.ppermute(head, axis, [((i + 1) % count, i) for i in range(ends)]),
            ],
            axis=dim,
        )
    return cells


def on_device(
    basis,
    near_blocks,
    near_list,
    source_basis,
    target_basis,
    coupling,
    far_target,
    far_source,
    far_count,
):
    basis_count = basis.shape[0]
    clusters = basis.shape[2]
    panels_cl = basis.shape[3]
    ranks = source_basis.shape[2]
    block_slots = coupling.shape[1]
    current = basis[basis_count - 1, 0]
    current_bf = current.astype(jnp.bfloat16)
    window = with_halo(current_bf, (("cl", 0),), clusters)
    gathered = window[near_list[0]]
    near_part = jnp.einsum(
        "tkij,tkj->ti", near_blocks[0], gathered, preferred_element_type=jnp.float32
    )
    expansion = jnp.einsum(
        "srp,sp->sr", source_basis[0], current_bf, preferred_element_type=jnp.float32
    ).astype(jnp.bfloat16)
    my_index = lax.axis_index("cl")
    slot_local = jnp.arange(block_slots, dtype=jnp.int32)
    my_sources = far_source[0]
    all_expansion = lax.all_gather(expansion, "cl", axis=0, tiled=True)
    picked = all_expansion[my_sources]
    square_blocks = coupling[0].reshape(block_slots, ranks, ranks)
    live_mask = (slot_local < far_count[0, 0]).astype(jnp.float32)
    contributions = (
        jnp.einsum("bij,bj->bi", square_blocks, picked, preferred_element_type=jnp.float32)
        * live_mask[:, None]
    )
    my_targets = lax.dynamic_slice_in_dim(far_target[0], my_index * block_slots, block_slots)
    row_ids = jnp.arange(clusters * lax.axis_size("cl"), dtype=jnp.int32)
    selector = (row_ids[:, None] == my_targets[None, :]).astype(jnp.float32)
    coupled = lax.psum_scatter(
        jnp.dot(selector, contributions, precision=lax.Precision.HIGHEST),
        "cl",
        scatter_dimension=0,
        tiled=True,
    )
    coupled_bf = coupled.astype(jnp.bfloat16)
    far_part = jnp.einsum(
        "tr,trp->tp", coupled_bf, target_basis[0], preferred_element_type=jnp.float32
    )
    image = 0.5 * current + near_part + far_part
    flat_basis = basis[:, 0].reshape(basis_count, clusters * panels_cl)
    flat_image = image.reshape(-1)
    panels = float(lax.axis_size("cl") * lax.axis_size("grp") * clusters * panels_cl)
    local_products = jnp.dot(flat_basis, flat_image, precision=lax.Precision.HIGHEST)
    gram_local = jnp.dot(flat_basis, flat_basis.T, precision=lax.Precision.HIGHEST)
    products, image_squares, gram_matrix = lax.psum(
        (local_products, jnp.sum(flat_image * flat_image), gram_local), ("cl", "grp")
    )
    projection = products / panels
    remainder = flat_image - jnp.dot(projection, flat_basis, precision=lax.Precision.HIGHEST)
    squares = (
        image_squares
        - 2.0 * jnp.sum(projection * products)
        + jnp.dot(
            projection,
            jnp.dot(gram_matrix, projection, precision=lax.Precision.HIGHEST),
            precision=lax.Precision.HIGHEST,
        )
    )
    new_norm = jnp.sqrt(squares / panels + 1e-06)
    next_vector = (remainder / new_norm).reshape(1, clusters, panels_cl)
    return (next_vector, jnp.concatenate([projection, new_norm[None]]))


def solution(mesh):
    placed = (
        P(None, "grp", "cl", None),
        P("grp", "cl", None, None, None),
        P("grp", "cl", None),
        P("grp", "cl", None, None),
        P("grp", "cl", None, None),
        P("grp", "cl", None),
        P("grp", None),
        P("grp", "cl"),
        P("grp", "cl"),
    )
    return jax.shard_map(
        on_device,
        mesh=mesh,
        in_specs=placed,
        out_specs=(P("grp", "cl", None), P()),
        check_vma=False,
    )
```

profile of v0, /device:TPU:14, one launch (start us, length us, event | category | flops | bytes accessed | tf_op | source)
XLA Modules:
  0.0 122.3 jit_solution(2837860129529427694)
XLA Ops:
  0.6 0.8 fusion.28
  1.4 3.4 %collective-permute-start = (bf16[8,128]{1,0:T(8,128)(2,1)S(1)}, bf16[8,128]{1,0:T(8,128)(2,1)S(1)}, u32[]{:S(2)}, u32[]{:S(2)}) collective-permute-start(bf16[8,128]{1,0:T(8,128)(2,1)S(1)} %get-tuple-element.7), channel_id=1, source_target_pairs={{0,4},{4,8},{8,12},{12,16},{16,20},{20,24},{24,28},{1,5},{5,9},{9,... | collective-permute-start | bytes 6152 | tf_op jit(solution)/shard_map/ppermute | solution.py:15
  4.9 2.4 %collective-permute-start.1 = (bf16[8,128]{1,0:T(8,128)(2,1)S(1)}, bf16[8,128]{1,0:T(8,128)(2,1)S(1)}, u32[]{:S(2)}, u32[]{:S(2)}) collective-permute-start(bf16[8,128]{1,0:T(8,128)(2,1)S(1)} %get-tuple-element.7), channel_id=1, source_target_pairs={{4,0},{8,4},{12,8},{16,12},{20,16},{24,20},{28,24},{5,1},{9,5},{13... | collective-permute-start | bytes 6152 | tf_op jit(solution)/shard_map/ppermute | solution.py:17
  7.3 0.7 copy-done.3
  8.1 1.0 fusion.9
  9.1 25.3 %all_gather.3 = bf16[64,32]{1,0:T(8,128)(2,1)S(1)} all-gather(bf16[8,32]{1,0:T(8,128)(2,1)S(1)} %convert_element_type.22), channel_id=1, replica_groups=mesh['cl'=8,'grp'=4] {'cl'}, dimensions={0}, use_global_device_ids=true | all-gather | bytes 4608 | tf_op jit(solution)/shard_map/all_gather | solution.py:53
  35.3 0.6 copy-done.6
  36.0 0.6 gather_fusion.1
  36.6 0.2 fusion.17
  36.7 0.2 fusion.14
  37.0 31.1 %all-reduce = bf16[64,32]{1,0:T(8,128)(2,1)S(1)} all-reduce(f32[64,32]{1,0:T(8,128)S(1)} %fusion.14), channel_id=2, replica_groups=mesh['cl'=8,'grp'=4] {'cl'}, use_global_device_ids=true, to_apply=%region_0.0.clone | all-reduce | flops 2048 | bytes 12288
  68.1 0.2 convolution_bitcast_fusion
  68.3 0.7 copy-done.7
  69.0 0.6 dynamic-slice.1
  70.4 0.6 gather_fusion
  71.0 0.4 fusion.1
  71.4 0.6 multiply_reduce_fusion
  72.0 0.1 convolution_bitcast_fusion.2
  72.2 45.3 %all-reduce.1 = (f32[16]{0:T(128)S(1)}, f32[]{:T(128)}, f32[16,16]{1,0:T(8,128)S(1)}) all-reduce(f32[16]{0:T(128)S(1)} %convolution_bitcast_fusion.2, f32[]{:T(128)} %get-tuple-element.5, f32[16,16]{1,0:T(8,128)S(1)} %convolution_bitcast_fusion), channel_id=1, replica_groups=mesh['cl'=8,'grp'=4] {'cl','grp'}, use_global_device_ids=true, to_apply=%region_1.0 | all-reduce | flops 273 | bytes 2184 | tf_op jit(solution)/shard_map/psum | solution.py:80
  117.5 0.6 broadcast_multiply_fusion
  118.1 0.2 fusion.4
  118.2 0.8 fusion.3
  121.1 0.6 fusion.21
  121.7 0.6 pad_maximum_fusion.1
  (28 shorter events, 0.6 us)
Async XLA Ops:
  0.6 70.4 %copy-start = (bf16[1,8,4,128,128]{4,3,2,1,0:T(8,128)(2,1)S(1)}, bf16[1,8,4,128,128]{4,3,2,1,0:T(8,128)(2,1)}, u32[]{:S(2)}) copy-start(bf16[1,8,4,128,128]{4,3,2,1,0:T(8,128)(2,1)} %param.10) | copy-start | bytes 3145732
  1.4 69.0 %collective-permute-start = (bf16[8,128]{1,0:T(8,128)(2,1)S(1)}, bf16[8,128]{1,0:T(8,128)(2,1)S(1)}, u32[]{:S(2)}, u32[]{:S(2)}) collective-permute-start(bf16[8,128]{1,0:T(8,128)(2,1)S(1)} %get-tuple-element.7), channel_id=1, source_target_pairs={{0,4},{4,8},{8,12},{12,16},{16,20},{20,24},{24,28},{1,5},{5,9},{9,... | collective-permute-start | bytes 6152 | tf_op jit(solution)/shard_map/ppermute | solution.py:15
  4.9 65.5 %collective-permute-start.1 = (bf16[8,128]{1,0:T(8,128)(2,1)S(1)}, bf16[8,128]{1,0:T(8,128)(2,1)S(1)}, u32[]{:S(2)}, u32[]{:S(2)}) collective-permute-start(bf16[8,128]{1,0:T(8,128)(2,1)S(1)} %get-tuple-element.7), channel_id=1, source_target_pairs={{4,0},{8,4},{12,8},{16,12},{20,16},{24,20},{28,24},{5,1},{9,5},{13... | collective-permute-start | bytes 6152 | tf_op jit(solution)/shard_map/ppermute | solution.py:17
  7.3 0.7 copy-start.3
  8.1 26.3 %copy-start.5 = (s32[1,16]{1,0:T(1,128)S(1)}, s32[1,16]{1,0:T(1,128)}, u32[]{:S(2)}) copy-start(s32[1,16]{1,0:T(1,128)} %param.16) | copy-start | bytes 196
  9.1 25.3 %copy-start.2 = (bf16[1,16,1024]{2,1,0:T(8,128)(2,1)S(1)}, bf16[1,16,1024]{2,1,0:T(8,128)(2,1)}, u32[]{:S(2)}) copy-start(bf16[1,16,1024]{2,1,0:T(8,128)(2,1)} %param.14) | copy-start | bytes 98308
  35.3 0.7 copy-start.6
  36.7 31.4 %copy-start.1 = (f32[16,1,8,128]{3,2,1,0:T(8,128)S(1)}, f32[16,1,8,128]{3,2,1,0:T(8,128)}, u32[]{:S(2)}) copy-start(f32[16,1,8,128]{3,2,1,0:T(8,128)} %param.9) | copy-start | bytes 196612
  37.0 33.3 %copy-start.4 = (bf16[1,8,32,128]{3,2,1,0:T(8,128)(2,1)S(1)}, bf16[1,8,32,128]{3,2,1,0:T(8,128)(2,1)}, u32[]{:S(2)}) copy-start(bf16[1,8,32,128]{3,2,1,0:T(8,128)(2,1)} %param.13) | copy-start | bytes 196612
  68.3 0.7 copy-start.7
where the time goes:
time: 123 us; the launch traced here: 122 us
  blocking collectives  102 us (83%)
  starting transfers between devices  5.83 us (5%)
  local copies, waits for them, and re-layouts  4.96 us (4%)
  between operations  4.13 us (3%)
  matrix products  3.17 us (3%)
  other arithmetic  2.44 us (2%)
    psum x1, blocking collectives, on_device(): lax.psum((local_products, jnp.sum(flat_image * flat_image), gram_local),...  45.3 us
    unnamed x1, blocking collectives  31.1 us
    all_gather x1, blocking collectives, on_device(): all_expansion = lax.all_gather(expansion, 'cl', axis=0, tiled=True)  25.3 us
    ppermute x1, starting transfers between devices, with_halo(): lax.ppermute(tail, axis, [(i, (i + 1) % count) for i in range(ends)])  3.44 us
    unnamed x17, local copies, waits for them, and re-layouts  2.63 us
  transfers between devices with their start and end apart: 2, of which 0 were waited for; matrix products, arithmetic and copies ran while one was open for 3% of the time, Pallas kernels for 0%

commit v1 on v0

--- a/solution.py
+++ b/solution.py
@@ -50,7 +50,9 @@
     my_index = lax.axis_index("cl")
     slot_local = jnp.arange(block_slots, dtype=jnp.int32)
     my_sources = far_source[0]
-    all_expansion = lax.all_gather(expansion, "cl", axis=0, tiled=True)
+    all_expansion = jnp.concatenate(
+        lax.all_to_all(jnp.stack([expansion] * lax.axis_size("cl")), "cl", 0, 0), axis=0
+    )
     picked = all_expansion[my_sources]
     square_blocks = coupling[0].reshape(block_slots, ranks, ranks)
     live_mask = (slot_local < far_count[0, 0]).astype(jnp.float32)

time: 123 us -> 105 us (0.85)
  blocking collectives: 102 us -> 76.6 us
  starting transfers between devices: 5.83 us -> 12 us
    all_gather x1 -> x0, blocking collectives: 25.3 us -> none  [on_device(): all_expansion = lax.all_gather(expansion, 'cl', axis=0, tiled=True)]
    all_to_all x0 -> x1, starting transfers between devices: none -> 6.22 us  [on_device(): lax.all_to_all(jnp.stack([expansion] * lax.axis_size('cl')), 'cl', 0, 0)]
    psum x1, blocking collectives: 45.3 us -> 46.7 us  [on_device(): lax.psum((local_products, jnp.sum(flat_image * flat_image), gram_local),...]
    unnamed x17 -> x19, local copies, waits for them, and re-layouts: 2.63 us -> 3.37 us
  transfers between devices with their start and end apart: 2 -> 3, of which waited for: 0 -> 0; matrix products, arithmetic and copies ran while one was open for 3% -> 4% of each run, Pallas kernels for 0% -> 0%
where the time goes in v1:
time: 105 us; the launch traced here: 104 us
  blocking collectives  76.6 us (73%)
  starting transfers between devices  12 us (11%)
  local copies, waits for them, and re-layouts  5.74 us (5%)
  between operations  4.09 us (4%)
  matrix products  3.11 us (3%)
  other arithmetic  2.43 us (2%)
    psum x1, blocking collectives, on_device(): lax.psum((local_products, jnp.sum(flat_image * flat_image), gram_local),...  46.7 us
    unnamed x1, blocking collectives  29.9 us
    all_to_all x1, starting transfers between devices, on_device(): lax.all_to_all(jnp.stack([expansion] * lax.axis_size('cl')), 'cl', 0, 0)  6.22 us
    ppermute x1, starting transfers between devices, with_halo(): lax.ppermute(tail, axis, [(i, (i + 1) % count) for i in range(ends)])  3.44 us
    unnamed x19, local copies, waits for them, and re-layouts  3.37 us
    ppermute x1, starting transfers between devices, with_halo(): lax.ppermute(head, axis, [((i + 1) % count, i) for i in range(ends)])  2.39 us
  transfers between devices with their start and end apart: 3, of which 0 were waited for; matrix products, arithmetic and copies ran while one was open for 4% of the time, Pallas kernels for 0%

profile of v1, /device:TPU:14, one launch (start us, length us, event | category | flops | bytes accessed | tf_op | source)
XLA Modules:
  0.0 104.0 jit_solution(4613057538775575945)
XLA Ops:
  0.6 0.8 fusion.28
  1.4 3.4 %collective-permute-start = (bf16[8,128]{1,0:T(8,128)(2,1)S(1)}, bf16[8,128]{1,0:T(8,128)(2,1)S(1)}, u32[]{:S(2)}, u32[]{:S(2)}) collective-permute-start(bf16[8,128]{1,0:T(8,128)(2,1)S(1)} %get-tuple-element.7), channel_id=1, source_target_pairs={{0,4},{4,8},{8,12},{12,16},{16,20},{20,24},{24,28},{1,5},{5,9},{9,... | collective-permute-start | bytes 6152 | tf_op jit(solution)/shard_map/ppermute | solution.py:15
  4.9 2.4 %collective-permute-start.1 = (bf16[8,128]{1,0:T(8,128)(2,1)S(1)}, bf16[8,128]{1,0:T(8,128)(2,1)S(1)}, u32[]{:S(2)}, u32[]{:S(2)}) collective-permute-start(bf16[8,128]{1,0:T(8,128)(2,1)S(1)} %get-tuple-element.7), channel_id=1, source_target_pairs={{4,0},{8,4},{12,8},{16,12},{20,16},{24,20},{28,24},{5,1},{9,5},{13... | collective-permute-start | bytes 6152 | tf_op jit(solution)/shard_map/ppermute | solution.py:17
  7.3 1.0 fusion.9
  8.3 0.7 reshape.125
  9.0 6.2 %all-to-all-start = ((bf16[8,2,128]{2,1,0:T(2,128)(2,1)}), bf16[8,2,128]{2,1,0:T(2,128)(2,1)S(1)}, u32[]{:S(2)}, u32[]{:S(2)}) async-start(bf16[8,2,128]{2,1,0:T(2,128)(2,1)} %reshape.125), calls=%async_computation | async-start | bytes 8192 | tf_op jit(solution)/shard_map/all_to_all | solution.py:54
  15.4 0.6 copy-done.5
  16.7 0.2 convolution_bitcast_fusion
  16.9 0.7 copy-done.6
  17.9 0.6 copy-done.7
  18.5 0.6 dynamic-slice.1
  19.8 0.6 gather_fusion
  20.4 0.4 fusion.1
  20.8 0.6 gather_fusion.1
  21.4 0.2 fusion.17
  21.6 0.2 fusion.14
  21.8 29.9 %all-reduce = bf16[64,32]{1,0:T(8,128)(2,1)S(1)} all-reduce(f32[64,32]{1,0:T(8,128)S(1)} %fusion.14), channel_id=2, replica_groups=mesh['cl'=8,'grp'=4] {'cl'}, use_global_device_ids=true, to_apply=%region_0.0.clone | all-reduce | flops 2048 | bytes 12288
  51.9 0.6 multiply_reduce_fusion
  52.7 46.7 %all-reduce.1 = (f32[16]{0:T(128)S(1)}, f32[]{:T(128)}, f32[16,16]{1,0:T(8,128)S(1)}) all-reduce(f32[16]{0:T(128)S(1)} %convolution_bitcast_fusion.2, f32[]{:T(128)} %get-tuple-element.5, f32[16,16]{1,0:T(8,128)S(1)} %convolution_bitcast_fusion), channel_id=1, replica_groups=mesh['cl'=8,'grp'=4] {'cl','grp'}, use_global_device_ids=true, to_apply=%region_1.0 | all-reduce | flops 273 | bytes 2184 | tf_op jit(solution)/shard_map/psum | solution.py:82
  99.3 0.6 broadcast_multiply_fusion
  99.9 0.2 fusion.4
  100.1 0.8 fusion.3
  102.8 0.6 fusion.21
  103.4 0.6 pad_maximum_fusion.1
  (32 shorter events, 0.9 us)
Async XLA Ops:
  0.6 19.7 %copy-start = (bf16[1,8,4,128,128]{4,3,2,1,0:T(8,128)(2,1)S(1)}, bf16[1,8,4,128,128]{4,3,2,1,0:T(8,128)(2,1)}, u32[]{:S(2)}) copy-start(bf16[1,8,4,128,128]{4,3,2,1,0:T(8,128)(2,1)} %param.10) | copy-start | bytes 3145732
  1.4 18.3 %collective-permute-start = (bf16[8,128]{1,0:T(8,128)(2,1)S(1)}, bf16[8,128]{1,0:T(8,128)(2,1)S(1)}, u32[]{:S(2)}, u32[]{:S(2)}) collective-permute-start(bf16[8,128]{1,0:T(8,128)(2,1)S(1)} %get-tuple-element.7), channel_id=1, source_target_pairs={{0,4},{4,8},{8,12},{12,16},{16,20},{20,24},{24,28},{1,5},{5,9},{9,... | collective-permute-start | bytes 6152 | tf_op jit(solution)/shard_map/ppermute | solution.py:15
  4.9 14.9 %collective-permute-start.1 = (bf16[8,128]{1,0:T(8,128)(2,1)S(1)}, bf16[8,128]{1,0:T(8,128)(2,1)S(1)}, u32[]{:S(2)}, u32[]{:S(2)}) collective-permute-start(bf16[8,128]{1,0:T(8,128)(2,1)S(1)} %get-tuple-element.7), channel_id=1, source_target_pairs={{4,0},{8,4},{12,8},{16,12},{20,16},{24,20},{28,24},{5,1},{9,5},{13... | collective-permute-start | bytes 6152 | tf_op jit(solution)/shard_map/ppermute | solution.py:17
  7.3 7.9 %copy-start.3 = (s32[1,8,4]{1,2,0:T(4,128)S(1)}, s32[1,8,4]{1,2,0:T(4,128)}, u32[]{:S(2)}) copy-start(s32[1,8,4]{1,2,0:T(4,128)} %param.11) | copy-start | bytes 388
  8.3 8.5 %copy-start.1 = (f32[16,1,8,128]{3,2,1,0:T(8,128)S(1)}, f32[16,1,8,128]{3,2,1,0:T(8,128)}, u32[]{:S(2)}) copy-start(f32[16,1,8,128]{3,2,1,0:T(8,128)} %param.9) | copy-start | bytes 196612
  9.0 11.8 %all-to-all-start = ((bf16[8,2,128]{2,1,0:T(2,128)(2,1)}), bf16[8,2,128]{2,1,0:T(2,128)(2,1)S(1)}, u32[]{:S(2)}, u32[]{:S(2)}) async-start(bf16[8,2,128]{2,1,0:T(2,128)(2,1)} %reshape.125), calls=%async_computation | async-start | bytes 8192 | tf_op jit(solution)/shard_map/all_to_all | solution.py:54
  15.4 0.7 copy-start.5
  16.7 1.0 copy-start.2
  16.9 0.7 copy-start.6
  17.8 0.7 copy-start.7
  21.6 30.2 %copy-start.4 = (bf16[1,8,32,128]{3,2,1,0:T(8,128)(2,1)S(1)}, bf16[1,8,32,128]{3,2,1,0:T(8,128)(2,1)}, u32[]{:S(2)}) copy-start(bf16[1,8,32,128]{3,2,1,0:T(8,128)(2,1)} %param.13) | copy-start | bytes 196612
